TPU v7x, 32 devices: a whole 2x2x4 slice. The times are simulated.
32 devices in a mesh: rep: 4 (over y, x), shard: 8 (over z, core).
Axes of the slice: x: 2, y: 2, z: 4, core: 2. Of those that a mesh axis runs over, the one named last changes fastest.
Arguments:
- latents_in: float32 [32, 256, 768], P(('rep', 'shard')), may hold values from -6 to 6
- conditioning: float32 [32, 768], P(('rep', 'shard')), may hold values from -6 to 6
- cotangent: float32 [32, 256, 768], P(('rep', 'shard')), may hold values from -6 to 6
- ada_weight: bfloat16 [768, 4608], P(None, 'shard'), may hold values from -0.21875 to 0.21875
- ada_bias: bfloat16 [4608], P('shard'), may hold values from -3 to 3
- qkv_weight: bfloat16 [768, 2304], P(None, 'shard'), may hold values from -0.21875 to 0.21875
- query_bias: bfloat16 [768], P('shard'), may hold values from -6 to 6
- value_bias: bfloat16 [768], P('shard'), may hold values from -6 to 6
- proj_weight: bfloat16 [768, 768], P(None, 'shard'), may hold values from -1.75 to 1.75
- proj_bias: bfloat16 [768], P('shard'), may hold values from -6 to 6
- fc1_weight: bfloat16 [768, 3072], P(None, 'shard'), may hold values from -0.21875 to 0.21875
- fc1_bias: bfloat16 [3072], P('shard'), may hold values from -6 to 6
- fc2_weight: bfloat16 [3072, 768], P(None, 'shard'), may hold values from -0.109375 to 0.109375
- fc2_bias: bfloat16 [768], P('shard'), may hold values from -6 to 6
Outputs:
- block_out: float32 [32, 256, 768], P(('rep', 'shard'))
- grad_input: float32 [32, 256, 768], P(('rep', 'shard'))
- grad_cond: float32 [32, 768], P(('rep', 'shard'))
- grad_ada_weight: float32 [768, 4608], P(None, 'shard')
- grad_ada_bias: float32 [4608], P('shard')
- grad_qkv_weight: float32 [768, 2304], P(None, 'shard')
- grad_query_bias: float32 [768], P('shard')
- grad_value_bias: float32 [768], P('shard')
- grad_proj_weight: float32 [768, 768], P(None, 'shard')
- grad_proj_bias: float32 [768], P('shard')
- grad_fc1_weight: float32 [768, 3072], P(None, 'shard')
- grad_fc1_bias: float32 [3072], P('shard')
- grad_fc2_weight: float32 [3072, 768], P(None, 'shard')
- grad_fc2_bias: float32 [768], P('shard')
All inputs are finite; a program needn't handle non-finite values.
Results may differ from a plain program's by a relative error of at most 0.01.
The roundings to bfloat16 on the way count: a program that leaves them out, or rounds other values in their place, can miss the bound.
Values may be sent and summed in bfloat16 or wider, within the bound.
No kernel may reach another device: no remote copies, remote signals or barrier semaphores. Data moves between devices by JAX's collectives and lax.ppermute only.
A program may use at most 192 MiB of HBM per device.

v0:
```python
import math
import jax
import jax.numpy as jnp
from jax import lax
from jax.sharding import PartitionSpec as P

HEAD = 64
gelu_scale = math.sqrt(2.0 / math.pi)
gelu_cubic = 0.044715
norm_eps = 1e-06


def layer_norm(values):
    center = values - jnp.mean(values, axis=-1, keepdims=True)
    variance = jnp.mean(center * center, axis=-1, keepdims=True)
    inv_std = lax.rsqrt(variance + norm_eps)
    return (center * inv_std, inv_std)


def norm_back(grad_normed, normed, inv_std):
    return inv_std * (
        grad_normed
        - jnp.mean(grad_normed, axis=-1, keepdims=True)
        - normed * jnp.mean(grad_normed * normed, axis=-1, keepdims=True)
    )


def head_product(form, left, right):
    return jnp.einsum(form, left, right, preferred_element_type=jnp.float32)


def flat_rows(values):
    return values.reshape(-1, values.shape[-1])


def matmul(left, right):
    return jnp.dot(left, right, preferred_element_type=jnp.float32)


def forward_all(latents, conds, weights):
    (
        ada_weight,
        ada_bias,
        qkv_weight,
        query_bias,
        value_bias,
        proj_weight,
        proj_bias,
        fc1_weight,
        fc1_bias,
        fc2_weight,
        fc2_bias,
    ) = weights
    count, seq_len, width = latents.shape
    head_count = width // HEAD
    sigmoid_c = jax.nn.sigmoid(conds)
    cond_act = (conds * sigmoid_c).astype(jnp.bfloat16)
    modulation = matmul(cond_act, ada_weight) + ada_bias.astype(jnp.float32)
    mods = [piece[:, None, :] for piece in jnp.split(modulation, 6, axis=1)]
    shift_one, scale_one, gate_one, shift_two, scale_two, gate_two = mods
    normed_one, inv_one = layer_norm(latents)
    hidden_one = (normed_one * (1.0 + scale_one) + shift_one).astype(jnp.bfloat16)
    qkv_rows = matmul(flat_rows(hidden_one), qkv_weight)
    head_shape = (count, seq_len, head_count, HEAD)
    query_heads = (
        (qkv_rows[:, :width] + query_bias.astype(jnp.float32))
        .astype(jnp.bfloat16)
        .reshape(head_shape)
    )
    key_heads = qkv_rows[:, width : 2 * width].astype(jnp.bfloat16).reshape(head_shape)
    value_heads = (
        (qkv_rows[:, 2 * width :] + value_bias.astype(jnp.float32))
        .astype(jnp.bfloat16)
        .reshape(head_shape)
    )
    scores = head_product("lqhd,lkhd->lhqk", query_heads, key_heads) * HEAD ** (-0.5)
    row_max = jnp.max(scores, axis=-1, keepdims=True)
    log_total = row_max + jnp.log(jnp.sum(jnp.exp(scores - row_max), axis=-1, keepdims=True))
    prob_low = jnp.exp(scores - log_total).astype(jnp.bfloat16)
    attended = (
        head_product("lhqk,lkhd->lqhd", prob_low, value_heads)
        .reshape(count, seq_len, width)
        .astype(jnp.bfloat16)
    )
    attn_out = (matmul(flat_rows(attended), proj_weight) + proj_bias.astype(jnp.float32)).reshape(
        count, seq_len, width
    )
    resid_mid = latents + gate_one * attn_out
    normed_two, inv_two = layer_norm(resid_mid)
    hidden_two = (normed_two * (1.0 + scale_two) + shift_two).astype(jnp.bfloat16)
    fc1_pre = (matmul(flat_rows(hidden_two), fc1_weight) + fc1_bias.astype(jnp.float32)).reshape(
        count, seq_len, -1
    )
    tanh_inner = jnp.tanh(gelu_scale * (fc1_pre + gelu_cubic * fc1_pre * fc1_pre * fc1_pre))
    fc1_act = (0.5 * fc1_pre * (1.0 + tanh_inner)).astype(jnp.bfloat16)
    mlp_out = (matmul(flat_rows(fc1_act), fc2_weight) + fc2_bias.astype(jnp.float32)).reshape(
        count, seq_len, width
    )
    block_out = resid_mid + gate_two * mlp_out
    saved = (
        conds,
        sigmoid_c,
        cond_act,
        modulation,
        normed_one,
        inv_one,
        hidden_one,
        query_heads,
        key_heads,
        value_heads,
        log_total,
        attended,
        attn_out,
        normed_two,
        inv_two,
        hidden_two,
        fc1_pre,
        tanh_inner,
        fc1_act,
        mlp_out,
    )
    return (block_out, saved)


def backward_all(cotangent, saved, weights, arrange):
    (
        ada_weight,
        ada_bias,
        qkv_weight,
        query_bias,
        value_bias,
        proj_weight,
        proj_bias,
        fc1_weight,
        fc1_bias,
        fc2_weight,
        fc2_bias,
    ) = weights
    (
        conds,
        sigmoid_c,
        cond_act,
        modulation,
        normed_one,
        inv_one,
        hidden_one,
        query_heads,
        key_heads,
        value_heads,
        log_total,
        attended,
        attn_out,
        normed_two,
        inv_two,
        hidden_two,
        fc1_pre,
        tanh_inner,
        fc1_act,
        mlp_out,
    ) = saved
    count, seq_len, width = attended.shape
    head_count = width // HEAD
    mods = [piece[:, None, :] for piece in jnp.split(modulation, 6, axis=1)]
    shift_one, scale_one, gate_one, shift_two, scale_two, gate_two = mods
    grad_gate_two = jnp.sum(cotangent * mlp_out, axis=1)
    grad_mlp = cotangent * gate_two
    grad_mlp_low = flat_rows(grad_mlp.astype(jnp.bfloat16))
    grad_fc2_bias = jnp.sum(flat_rows(grad_mlp), axis=0)
    grad_fc2 = matmul(flat_rows(fc1_act).T, arrange(grad_mlp_low))
    grad_act = matmul(grad_mlp_low, fc2_weight.T).reshape(fc1_pre.shape)
    slope = 0.5 * (1.0 + tanh_inner) + 0.5 * fc1_pre * (
        1.0 - tanh_inner * tanh_inner
    ) * gelu_scale * (1.0 + 3.0 * gelu_cubic * fc1_pre * fc1_pre)
    grad_pre = grad_act * slope
    grad_pre_low = flat_rows(grad_pre.astype(jnp.bfloat16))
    grad_fc1_bias = jnp.sum(flat_rows(grad_pre), axis=0)
    grad_fc1 = matmul(flat_rows(hidden_two).T, arrange(grad_pre_low))
    grad_hidden_two = matmul(grad_pre_low, fc1_weight.T).reshape(count, seq_len, width)
    grad_shift_two = jnp.sum(grad_hidden_two, axis=1)
    grad_scale_two = jnp.sum(grad_hidden_two * normed_two, axis=1)
    grad_mid = cotangent + norm_back(grad_hidden_two * (1.0 + scale_two), normed_two, inv_two)
    grad_gate_one = jnp.sum(grad_mid * attn_out, axis=1)
    grad_attn = grad_mid * gate_one
    grad_attn_low = flat_rows(grad_attn.astype(jnp.bfloat16))
    grad_proj_bias = jnp.sum(flat_rows(grad_attn), axis=0)
    grad_proj = matmul(flat_rows(attended).T, arrange(grad_attn_low))
    head_shape = (count, seq_len, head_count, HEAD)
    grad_attended = matmul(grad_attn_low, proj_weight.T).astype(jnp.bfloat16).reshape(head_shape)
    scores = head_product("lqhd,lkhd->lhqk", query_heads, key_heads) * HEAD ** (-0.5)
    prob_full = jnp.exp(scores - log_total)
    prob_low = prob_full.astype(jnp.bfloat16)
    grad_value = head_product("lhqk,lqhd->lkhd", prob_low, grad_attended).reshape(
        count * seq_len, width
    )
    grad_prob = head_product("lqhd,lkhd->lhqk", grad_attended, value_heads)
    row_delta = jnp.sum(prob_full * grad_prob, axis=-1, keepdims=True)
    grad_scores = (prob_full * (grad_prob - row_delta) * HEAD ** (-0.5)).astype(jnp.bfloat16)
    grad_query = head_product("lhqk,lkhd->lqhd", grad_scores, key_heads).reshape(
        count * seq_len, width
    )
    grad_key = head_product("lhqk,lqhd->lkhd", grad_scores, query_heads).reshape(
        count * seq_len, width
    )
    grad_query_bias = jnp.sum(grad_query, axis=0)
    grad_value_bias = jnp.sum(grad_value, axis=0)
    grad_qkv_low = jnp.concatenate([grad_query, grad_key, grad_value], axis=1).astype(jnp.bfloat16)
    grad_qkv = matmul(flat_rows(hidden_one).T, arrange(grad_qkv_low))
    grad_hidden_one = matmul(grad_qkv_low, qkv_weight.T).reshape(count, seq_len, width)
    grad_shift_one = jnp.sum(grad_hidden_one, axis=1)
    grad_scale_one = jnp.sum(grad_hidden_one * normed_one, axis=1)
    grad_latent = grad_mid + norm_back(grad_hidden_one * (1.0 + scale_one), normed_one, inv_one)
    grad_mod = jnp.concatenate(
        [
            grad_shift_one,
            grad_scale_one,
            grad_gate_one,
            grad_shift_two,
            grad_scale_two,
            grad_gate_two,
        ],
        axis=1,
    )
    grad_mod_low = grad_mod.astype(jnp.bfloat16)
    grad_ada = matmul(cond_act.T, arrange(grad_mod_low))
    grad_cond_row = matmul(grad_mod_low, ada_weight.T)
    grad_cond = grad_cond_row * sigmoid_c * (1.0 + conds * (1.0 - sigmoid_c))
    grads = (
        grad_ada,
        arrange(jnp.sum(grad_mod, axis=0)),
        grad_qkv,
        arrange(grad_query_bias),
        arrange(grad_value_bias),
        grad_proj,
        arrange(grad_proj_bias),
        grad_fc1,
        arrange(grad_fc1_bias),
        grad_fc2,
        arrange(grad_fc2_bias),
    )
    return (grad_latent, grad_cond, grads)


def keep_order(values):
    return values


def local(
    latents_in,
    conditioning,
    cotangent,
    ada_weight,
    ada_bias,
    qkv_weight,
    query_bias,
    value_bias,
    proj_weight,
    proj_bias,
    fc1_weight,
    fc1_bias,
    fc2_weight,
    fc2_bias,
):
    weights_fwd = (
        lax.all_gather(ada_weight, "shard", axis=1, tiled=True),
        lax.all_gather(ada_bias, "shard", axis=0, tiled=True),
        lax.all_gather(qkv_weight, "shard", axis=1, tiled=True),
        lax.all_gather(query_bias, "shard", axis=0, tiled=True),
        lax.all_gather(value_bias, "shard", axis=0, tiled=True),
        lax.all_gather(proj_weight, "shard", axis=1, tiled=True),
        lax.all_gather(proj_bias, "shard", axis=0, tiled=True),
        lax.all_gather(fc1_weight, "shard", axis=1, tiled=True),
        lax.all_gather(fc1_bias, "shard", axis=0, tiled=True),
        lax.all_gather(fc2_weight, "shard", axis=1, tiled=True),
        lax.all_gather(fc2_bias, "shard", axis=0, tiled=True),
    )
    block_out, saved_all = forward_all(latents_in, conditioning, weights_fwd)
    weights_bwd = (
        lax.all_gather(ada_weight, "shard", axis=1, tiled=True),
        lax.all_gather(ada_bias, "shard", axis=0, tiled=True),
        lax.all_gather(qkv_weight, "shard", axis=1, tiled=True),
        lax.all_gather(query_bias, "shard", axis=0, tiled=True),
        lax.all_gather(value_bias, "shard", axis=0, tiled=True),
        lax.all_gather(proj_weight, "shard", axis=1, tiled=True),
        lax.all_gather(proj_bias, "shard", axis=0, tiled=True),
        lax.all_gather(fc1_weight, "shard", axis=1, tiled=True),
        lax.all_gather(fc1_bias, "shard", axis=0, tiled=True),
        lax.all_gather(fc2_weight, "shard", axis=1, tiled=True),
        lax.all_gather(fc2_bias, "shard", axis=0, tiled=True),
    )
    grad_input, grad_cond, totals = backward_all(cotangent, saved_all, weights_bwd, keep_order)
    group_sums = (
        lax.psum_scatter(totals[0], "shard", scatter_dimension=1, tiled=True),
        lax.psum_scatter(totals[1], "shard", scatter_dimension=0, tiled=True),
        lax.psum_scatter(totals[2], "shard", scatter_dimension=1, tiled=True),
        lax.psum_scatter(totals[3], "shard", scatter_dimension=0, tiled=True),
        lax.psum_scatter(totals[4], "shard", scatter_dimension=0, tiled=True),
        lax.psum_scatter(totals[5], "shard", scatter_dimension=1, tiled=True),
        lax.psum_scatter(totals[6], "shard", scatter_dimension=0, tiled=True),
        lax.psum_scatter(totals[7], "shard", scatter_dimension=1, tiled=True),
        lax.psum_scatter(totals[8], "shard", scatter_dimension=0, tiled=True),
        lax.psum_scatter(totals[9], "shard", scatter_dimension=1, tiled=True),
        lax.psum_scatter(totals[10], "shard", scatter_dimension=0, tiled=True),
    )
    finals = lax.psum(
        (
            group_sums[0],
            group_sums[1],
            group_sums[2],
            group_sums[3],
            group_sums[4],
            group_sums[5],
            group_sums[6],
            group_sums[7],
            group_sums[8],
            group_sums[9],
            group_sums[10],
        ),
        "rep",
    )
    return (
        block_out,
        grad_input,
        grad_cond,
        finals[0],
        finals[1],
        finals[2],
        finals[3],
        finals[4],
        finals[5],
        finals[6],
        finals[7],
        finals[8],
        finals[9],
        finals[10],
    )


def solution(mesh):
    placed = (
        P(("rep", "shard"), None, None),
        P(("rep", "shard"), None),
        P(("rep", "shard"), None, None),
        P(None, "shard"),
        P("shard"),
        P(None, "shard"),
        P("shard"),
        P("shard"),
        P(None, "shard"),
        P("shard"),
        P(None, "shard"),
        P("shard"),
        P(None, "shard"),
        P("shard"),
    )
    return jax.shard_map(
        local,
        mesh=mesh,
        in_specs=placed,
        out_specs=(
            P(("rep", "shard"), None, None),
            P(("rep", "shard"), None, None),
            P(("rep", "shard"), None),
            P(None, "shard"),
            P("shard"),
            P(None, "shard"),
            P("shard"),
            P("shard"),
            P(None, "shard"),
            P("shard"),
            P(None, "shard"),
            P("shard"),
            P(None, "shard"),
            P("shard"),
        ),
        check_vma=False,
    )
```

profile of v0, /device:TPU:0, one launch (start us, length us, event | category | flops | bytes accessed | tf_op | source)
XLA Modules:
  0.0 869.6 jit_solution(10159185323933018458)
XLA Ops:
  17.5 32.6 %all-reduce.14 = (bf16[4608]{0:T(1024)(128)(2,1)S(1)}, bf16[768]{0:T(1024)(128)(2,1)S(1)}, bf16[768]{0:T(1024)(128)(2,1)S(1)}, bf16[768]{0:T(1024)(128)(2,1)S(1)}, bf16[768]{0:T(1024)(128)(2,1)S(1)}) all-reduce(bf16[4608]{0:T(1024)(128)(2,1)S(1)} %dynamic-update-slice, ...), channel_id=1, replica_groups=mesh['rep'=4,'shard'=8] {'shard'}, use_global_device_ids=true, to_apply=%add | all-reduce | flops 7680 | bytes 30720
  51.3 13.4 %all-gather = bf16[8,1,384]{2,1,0:T(2,128)(2,1)S(1)} all-gather(bf16[1,1,384]{2,1,0:T(2,128)(2,1)S(1)} %reshape.412), channel_id=1, replica_groups=mesh['rep'=4,'shard'=8] {'shard'}, dimensions={0}, use_global_device_ids=true | all-gather | bytes 6912 | tf_op jit(solution)/shard_map/all_gather | solution.py:272
  66.3 17.9 %all-gather.7.cloned.1.call-done = bf16[768,4608]{0,1:T(8,128)(2,1)} async-done(((bf16[768,576]{0,1:T(8,128)(2,1)}), bf16[768,4608]{0,1:T(8,128)(2,1)}) %all-gather.7.cloned.1.call-update) | async-done | bytes 7077904 | tf_op jit(solution)/shard_map/all_gather | solution.py:264
  84.2 5.0 convolution_reduce_fusion
  89.8 36.1 %all-gather.9.cloned.1.call-done = bf16[768,2304]{0,1:T(8,128)(2,1)} async-done(((bf16[768,288]{0,1:T(8,128)(2,1)}), bf16[768,2304]{0,1:T(8,128)(2,1)}) %all-gather.9.cloned.1.call-update) | async-done | bytes 3538960 | tf_op jit(solution)/shard_map/all_gather | solution.py:266
  134.9 14.3 %all-gather.11.cloned.1.call-done = bf16[768,768]{0,1:T(8,128)(2,1)} async-done(((bf16[768,96]{0,1:T(8,128)(2,1)}), bf16[768,768]{0,1:T(8,128)(2,1)}) %all-gather.11.cloned.1.call-update) | async-done | bytes 1179664 | tf_op jit(solution)/shard_map/all_gather | solution.py:269
  153.8 48.0 %all-gather.13.cloned.1.call-done = bf16[768,3072]{1,0:T(8,128)(2,1)} async-done(((bf16[768,384]{1,0:T(8,128)(2,1)}), bf16[768,3072]{1,0:T(8,128)(2,1)}) %all-gather.13.cloned.1.call-update) | async-done | bytes 4718608 | tf_op jit(solution)/shard_map/all_gather | solution.py:271
  201.7 5.8 convolution_add_fusion
  207.5 45.6 %all-gather.15.cloned.1.call-done = bf16[3072,768]{0,1:T(8,128)(2,1)} async-done(((bf16[3072,96]{0,1:T(8,128)(2,1)}), bf16[3072,768]{0,1:T(8,128)(2,1)}) %all-gather.15.cloned.1.call-update) | async-done | bytes 4718608 | tf_op jit(solution)/shard_map/all_gather | solution.py:273
  253.1 7.2 fusion.84
  279.6 5.2 fusion.21
  284.8 5.8 fusion.80
  293.7 4.1 fusion.41
  299.5 5.1 fusion.37
  306.5 6.3 fusion.52
  319.4 6.0 broadcast_multiply_fusion
  325.6 60.3 %reduce-scatter.8.cloned.1.call-done = f32[768,288]{0,1:T(8,128)} async-done(((f32[768,2304]{0,1:T(8,128)}), f32[768,288]{0,1:T(8,128)}) %reduce-scatter.8.cloned.1.call-update) | async-done | bytes 884752 | tf_op jit(solution)/shard_map/reduce_scatter | solution.py:294
  385.9 100.2 %reduce-scatter.12.cloned.1.call-done = f32[768,384]{1,0:T(8,128)} async-done(((f32[768,3072]{1,0:T(8,128)}), f32[768,384]{1,0:T(8,128)}) %reduce-scatter.12.cloned.1.call-update) | async-done | bytes 1179664 | tf_op jit(solution)/shard_map/reduce_scatter | solution.py:299
  486.2 100.2 %reduce-scatter.14.cloned.1.call-done = f32[3072,96]{0,1:T(8,128)} async-done(((f32[3072,768]{0,1:T(8,128)}), f32[3072,96]{0,1:T(8,128)}) %reduce-scatter.14.cloned.1.call-update) | async-done | bytes 1179664 | tf_op jit(solution)/shard_map/reduce_scatter | solution.py:301
  586.4 144.6 %reduce-scatter.6.cloned.1.call-done = f32[768,576]{0,1:T(8,128)} async-done(((f32[768,4608]{0,1:T(8,128)}), f32[768,576]{0,1:T(8,128)}) %reduce-scatter.6.cloned.1.call-update) | async-done | bytes 1769488 | tf_op jit(solution)/shard_map/reduce_scatter | solution.py:292
  733.3 26.4 %all-reduce.11 = (f32[4608]{0:T(1024)S(1)}, f32[768]{0:T(1024)S(1)}, f32[768]{0:T(1024)S(1)}, f32[768]{0:T(1024)S(1)}, f32[3072]{0:T(1024)S(1)}, /*index=5*/f32[768]{0:T(1024)S(1)}) all-reduce(f32[4608]{0:T(1024)S(1)} %reduce.38, f32[768]{0:T(1024)S(1)} %reduce_sum.235, ...), channel_id=3, replica_groups=mesh['rep'=4,'shard'=8] {'shard'}, use_global_device_ids=true, to_apply=%region_19.0.clone | all-reduce | flops 10752 | bytes 86016
  760.2 11.3 %all-reduce.12 = (f32[576]{0:T(1024)}, f32[96]{0:T(128)}, f32[96]{0:T(128)}, f32[96]{0:T(128)}, f32[384]{0:T(512)}, /*index=5*/f32[96]{0:T(128)}) all-reduce(f32[576]{0:T(1024)S(1)} %dynamic-slice.6, f32[96]{0:T(128)S(1)} %dynamic-slice.8, f32[96]{0:T(128)S(1)} %dynamic-slice.10, ...), channel_id=1, replica_groups=mesh['rep'=4,'shard'=8] {'rep'}, use_global_device_ids=true, to_apply=%region_20.0 | all-reduce | flops 1344 | bytes 10752 | tf_op jit(solution)/shard_map/psum | solution.py:304
  772.7 4.6 fusion.24
  777.3 79.2 %all-reduce.17.cloned.1.call-done = (f32[768,576]{0,1:T(8,128)}, f32[768,288]{0,1:T(8,128)}, f32[768,96]{0,1:T(8,128)}, f32[768,384]{1,0:T(8,128)}, f32[3072,96]{0,1:T(8,128)}) async-done(((f32[768,576]{0,1:T(8,128)}, f32[768,288]{0,1:T(8,128)}, f32[768,96]{0,1:T(8,128)}, f32[768,384]{1,0:T(8,128)}, f32[3072,96]{0,1:T(8,128)}), (f32[768,576]{0,1:T(8,128)}, f32[768,288]{0,1:T(8,128)}, f32[768,96]{0,1:T(8,128)}, ...) | async-done | bytes 5308432 | tf_op jit(solution)/shard_map/psum | solution.py:304
  (226 shorter events, 66.6 us)
Async XLA Ops:
  7.2 58.7 %copy-start = (f32[1,256,768]{2,1,0:T(8,128)S(1)}, f32[1,256,768]{2,1,0:T(8,128)}, u32[]{:S(2)}) copy-start(f32[1,256,768]{2,1,0:T(8,128)} %param.14) | copy-start | bytes 2359300
  7.2 77.0 %copy-start.38 = (f32[1,768]{1,0:T(1,128)S(1)}, f32[1,768]{1,0:T(1,128)}, u32[]{:S(2)}) copy-start(f32[1,768]{1,0:T(1,128)} %param.15) | copy-start | bytes 9220
  7.2 77.0 %all-gather.7.cloned.1.call-start = ((), (), s32[]{:S(2)}) async-start(), calls=%async_computation.5 | async-start | bytes 7962624 | tf_op jit(solution)/shard_map/all_gather | solution.py:264
  7.9 117.9 %all-gather.9.cloned.1.call-start = ((), (), s32[]{:S(2)}) async-start(), calls=%async_computation.6 | async-start | bytes 3981312 | tf_op jit(solution)/shard_map/all_gather | solution.py:266
  8.7 140.5 %all-gather.11.cloned.1.call-start = ((), (), s32[]{:S(2)}) async-start(), calls=%async_computation.7 | async-start | bytes 1327104 | tf_op jit(solution)/shard_map/all_gather | solution.py:269
  9.4 192.3 %all-gather.13.cloned.1.call-start = ((), (), s32[]{:S(2)}) async-start(), calls=%async_computation.8 | async-start | bytes 5308416 | tf_op jit(solution)/shard_map/all_gather | solution.py:271
  10.0 243.1 %all-gather.15.cloned.1.call-start = ((), (), s32[]{:S(2)}) async-start(), calls=%async_computation.9 | async-start | bytes 5308416 | tf_op jit(solution)/shard_map/all_gather | solution.py:273
  10.6 315.0 %reduce-scatter.10.cloned.1.call-start = ((), (), s32[]{:S(2)}) async-start(), calls=%async_computation.12 | async-start | bytes 2654208 | tf_op jit(solution)/shard_map/reduce_scatter | solution.py:297
  66.0 59.8 %copy-start.29 = (f32[256]{0:T(256)}, f32[256]{0:T(256)S(1)}, u32[]{:S(2)}) copy-start(f32[256]{0:T(256)S(1)} %broadcast_multiply_fusion.6) | copy-start | bytes 3076
  66.3 59.6 %copy-start.33 = (f32[256]{0:T(256)}, f32[256]{0:T(256)S(1)}, u32[]{:S(2)}) copy-start(f32[256]{0:T(256)S(1)} %add_rsqrt_fusion.1) | copy-start | bytes 3076
  253.1 7.2 copy-start.46
  253.1 7.2 copy-start.49
  253.1 7.2 copy-start.56
  271.5 114.4 %reduce-scatter.8.cloned.1.call-start = ((), (), s32[]{:S(2)}) async-start(), calls=%async_computation.11 | async-start | bytes 7962624 | tf_op jit(solution)/shard_map/reduce_scatter | solution.py:294
  297.8 188.3 %reduce-scatter.12.cloned.1.call-start = ((), (), s32[]{:S(2)}) async-start(), calls=%async_computation.13 | async-start | bytes 10616832 | tf_op jit(solution)/shard_map/reduce_scatter | solution.py:299
  304.6 281.8 %reduce-scatter.14.cloned.1.call-start = ((), (), s32[]{:S(2)}) async-start(), calls=%async_computation.14 | async-start | bytes 10616832 | tf_op jit(solution)/shard_map/reduce_scatter | solution.py:301
  312.9 418.2 %reduce-scatter.6.cloned.1.call-start = ((), (), s32[]{:S(2)}) async-start(), calls=%async_computation.10 | async-start | bytes 15925248 | tf_op jit(solution)/shard_map/reduce_scatter | solution.py:292
  325.5 407.6 %copy-start.51 = (f32[12,64]{1,0:T(8,128)S(1)}, f32[12,64]{1,0:T(8,128)}, u32[]{:S(2)}) copy-start(f32[12,64]{1,0:T(8,128)} %get-tuple-element.65) | copy-start | bytes 9220
  325.5 407.6 %copy-start.37 = (f32[12,64]{1,0:T(8,128)S(1)}, f32[12,64]{1,0:T(8,128)}, u32[]{:S(2)}) copy-start(f32[12,64]{1,0:T(8,128)} %get-tuple-element.63) | copy-start | bytes 9220
  325.5 407.8 %copy-start.48 = (f32[3072]{0:T(1024)S(1)}, f32[3072]{0:T(1024)}, u32[]{:S(2)}) copy-start(f32[3072]{0:T(1024)} %get-tuple-element.76) | copy-start | bytes 36868
  325.5 407.8 %copy-start.52 = (f32[768]{0:T(1024)S(1)}, f32[768]{0:T(1024)}, u32[]{:S(2)}) copy-start(f32[768]{0:T(1024)} %get-tuple-element.18) | copy-start | bytes 9220
  325.5 407.8 %copy-start.53 = (f32[768]{0:T(1024)S(1)}, f32[768]{0:T(1024)}, u32[]{:S(2)}) copy-start(f32[768]{0:T(1024)} %get-tuple-element.61) | copy-start | bytes 9220
  325.5 446.0 %copy-start.4 = (f32[1,256,768]{2,1,0:T(8,128)S(1)}, f32[1,256,768]{2,1,0:T(8,128)}, u32[]{:S(2)}) copy-start(f32[1,256,768]{2,1,0:T(8,128)} %copy-done.3) | copy-start | bytes 2359300
  325.5 530.9 %all-reduce.17.cloned.1.call-start = ((), (), s32[]{:S(2)}) async-start(), calls=%async_computation.15 | async-start | bytes 10616832 | tf_op jit(solution)/shard_map/psum | solution.py:304
  (44 other events, 114.6 us)
Sparse Core Ops, SparseCore 0:
  9.7 74.4 all-gather.6
  85.8 40.0 all-gather.8
  127.5 21.6 all-gather.10
  150.6 51.0 all-gather.12
  203.2 49.8 all-gather.14
  271.6 35.7 reduce-scatter.9
  309.8 76.0 reduce-scatter.7
  388.2 97.8 reduce-scatter.11
  488.5 97.8 reduce-scatter.13
  588.6 142.4 reduce-scatter.5
  735.3 121.1 all-reduce.16
where the time goes:
time: 870 us
  waiting for transfers between devices  650 us (75%)
  blocking collectives  83.6 us (10%)
  matrix products  77.6 us (9%)
  local copies, waits for them, and re-layouts  27.8 us (3%)
  between operations  17.7 us (2%)
  other arithmetic  12.4 us (1%)
    reduce_scatter x1, waiting for transfers between devices, local(): lax.psum_scatter(totals[0], 'shard', scatter_dimension=1, tiled=True)  145 us
    reduce_scatter x1, waiting for transfers between devices, local(): lax.psum_scatter(totals[9], 'shard', scatter_dimension=1, tiled=True)  100 us
    reduce_scatter x1, waiting for transfers between devices, local(): lax.psum_scatter(totals[7], 'shard', scatter_dimension=1, tiled=True)  100 us
    psum x1, waiting for transfers between devices, local(): lax.psum((group_sums[0], group_sums[1], group_sums[2], group_sums[3], gro...  79.2 us
    reduce_scatter x1, waiting for transfers between devices, local(): lax.psum_scatter(totals[2], 'shard', scatter_dimension=1, tiled=True)  60.3 us
    unnamed x2, blocking collectives  58.9 us
    dot_general x14, matrix products, matmul(): return jnp.dot(left, right, preferred_element_type=jnp.float32)  58.6 us
    all_gather x1, waiting for transfers between devices, local(): lax.all_gather(fc1_weight, 'shard', axis=1, tiled=True)  48 us
  transfers between devices with their start and end apart: 11, of which 10 were waited for; matrix products, arithmetic and copies ran while one was open for 10% of the time, Pallas kernels for 0%

commit v1 on v0

--- a/solution.py
+++ b/solution.py
@@ -8,6 +8,33 @@
 gelu_scale = math.sqrt(2.0 / math.pi)
 gelu_cubic = 0.044715
 norm_eps = 1e-06
+
+
+def _build_slots(slab_in, where_dim):
+    slab_in = jnp.moveaxis(slab_in, 0, where_dim)
+    g_now = slab_in.shape
+    return slab_in.reshape(
+        *g_now[:where_dim], g_now[where_dim] * g_now[where_dim + 1], *g_now[where_dim + 2 :]
+    )
+
+
+def pack_circles_over_axis(unit, net_axis):
+    arr_out = unit[None]
+    amount_of = lax.axis_size(net_axis)
+    for idx in range(amount_of.bit_length() - 1):
+        row_out = 1 << idx
+        pages = []
+        for src_i in range(amount_of):
+            pages.append((src_i, src_i ^ row_out))
+        front = lax.ppermute(arr_out, net_axis, pages)
+        aux = jnp.stack([arr_out, front])
+        low = lax.axis_index(net_axis) >> idx & 1
+        arr_out = jnp.where(low == 0, aux, aux[::-1]).reshape(-1, *unit.shape)
+    return arr_out
+
+
+def modes_view(view, x_part, at_axis):
+    return _build_slots(pack_circles_over_axis(view, x_part), at_axis)
 
 
 def layer_norm(values):
@@ -268,7 +295,7 @@
         lax.all_gather(value_bias, "shard", axis=0, tiled=True),
         lax.all_gather(proj_weight, "shard", axis=1, tiled=True),
         lax.all_gather(proj_bias, "shard", axis=0, tiled=True),
-        lax.all_gather(fc1_weight, "shard", axis=1, tiled=True),
+        modes_view(fc1_weight, "shard", 1),
         lax.all_gather(fc1_bias, "shard", axis=0, tiled=True),
         lax.all_gather(fc2_weight, "shard", axis=1, tiled=True),
         lax.all_gather(fc2_bias, "shard", axis=0, tiled=True),

time: 870 us -> 958 us (1.10)
  blocking collectives: 83.6 us -> 203 us
  waiting for transfers between devices: 650 us -> 597 us
    unnamed x2, blocking collectives: 58.9 us -> 178 us
    ppermute x0 -> x3, waiting for transfers between devices: none -> 77 us  [pack_circles_over_axis(): front = lax.ppermute(arr_out, net_axis, pages)]
    all_gather x1, waiting for transfers between devices: 45.6 us -> 0.01 us  [local(): lax.all_gather(fc2_weight, 'shard', axis=1, tiled=True)]
    all_gather x1, waiting for transfers between devices: 36.1 us -> 0.01 us  [local(): lax.all_gather(qkv_weight, 'shard', axis=1, tiled=True)]
    all_gather x1, waiting for transfers between devices: 17.9 us -> 0.01 us  [local(): lax.all_gather(ada_weight, 'shard', axis=1, tiled=True)]
    all_gather x1, waiting for transfers between devices: 48 us -> 32.8 us  [local(): lax.all_gather(fc1_weight, 'shard', axis=1, tiled=True)]
    all_gather x1, waiting for transfers between devices: 14.3 us -> 0.02 us  [local(): lax.all_gather(proj_weight, 'shard', axis=1, tiled=True)]
    unnamed x147 -> x159, local copies, waits for them, and re-layouts: 23.5 us -> 17.5 us
  transfers between devices with their start and end apart: 11 -> 14, of which waited for: 10 -> 8; matrix products, arithmetic and copies ran while one was open for 10% -> 11% of each run, Pallas kernels for 0% -> 0%
where the time goes in v1:
time: 958 us; the launch traced here: 957 us
  waiting for transfers between devices  597 us (62%)
  blocking collectives  203 us (21%)
  matrix products  84.1 us (9%)
  local copies, waits for them, and re-layouts  27.1 us (3%)
  other arithmetic  20.2 us (2%)
  between operations  17.8 us (2%)
    unnamed x2, blocking collectives  178 us
    reduce_scatter x1, waiting for transfers between devices, local(): lax.psum_scatter(totals[0], 'shard', scatter_dimension=1, tiled=True)  145 us
    reduce_scatter x1, waiting for transfers between devices, local(): lax.psum_scatter(totals[9], 'shard', scatter_dimension=1, tiled=True)  100 us
    reduce_scatter x1, waiting for transfers between devices, local(): lax.psum_scatter(totals[7], 'shard', scatter_dimension=1, tiled=True)  100 us
    psum x1, waiting for transfers between devices, local(): lax.psum((group_sums[0], group_sums[1], group_sums[2], group_sums[3], gro...  79.2 us
    ppermute x3, waiting for transfers between devices, pack_circles_over_axis(): front = lax.ppermute(arr_out, net_axis, pages)  77 us
    dot_general x14, matrix products, matmul(): return jnp.dot(left, right, preferred_element_type=jnp.float32)  65.1 us
    reduce_scatter x1, waiting for transfers between devices, local(): lax.psum_scatter(totals[2], 'shard', scatter_dimension=1, tiled=True)  60.3 us
  transfers between devices with their start and end apart: 14, of which 8 were waited for; matrix products, arithmetic and copies ran while one was open for 11% of the time, Pallas kernels for 0%

profile of v1, /device:TPU:0, one launch (start us, length us, event | category | flops | bytes accessed | tf_op | source)
XLA Modules:
  0.0 957.0 jit_solution(5799851253252892337)
XLA Ops:
  17.0 75.1 %collective-permute-done.1 = bf16[2,768,384]{2,1,0:T(8,128)(2,1)S(1)} collective-permute-done((bf16[2,768,384]{2,1,0:T(8,128)(2,1)S(1)}, bf16[2,768,384]{2,1,0:T(8,128)(2,1)S(1)}, u32[]{:S(2)}, u32[]{:S(2)}) %collective-permute-start.1) | collective-permute-done | bytes 1179680 | tf_op jit(solution)/shard_map/ppermute | solution.py:29
  102.2 151.7 %all-reduce.14 = (bf16[4608]{0:T(1024)(128)(2,1)S(1)}, bf16[768]{0:T(1024)(128)(2,1)S(1)}, bf16[768]{0:T(1024)(128)(2,1)S(1)}, bf16[768]{0:T(1024)(128)(2,1)S(1)}, bf16[768]{0:T(1024)(128)(2,1)S(1)}) all-reduce(bf16[4608]{0:T(1024)(128)(2,1)S(1)} %dynamic-update-slice, ...), channel_id=1, replica_groups=mesh['rep'=4,'shard'=8] {'shard'}, use_global_device_ids=true, to_apply=%add | all-reduce | flops 7680 | bytes 30720
  254.6 13.4 %all-gather = bf16[8,1,384]{2,1,0:T(2,128)(2,1)S(1)} all-gather(bf16[1,1,384]{2,1,0:T(2,128)(2,1)S(1)} %reshape.428), channel_id=1, replica_groups=mesh['rep'=4,'shard'=8] {'shard'}, dimensions={0}, use_global_device_ids=true | all-gather | bytes 6912 | tf_op jit(solution)/shard_map/all_gather | solution.py:299
  278.3 5.0 convolution_reduce_fusion
  296.9 5.7 convolution_add_fusion
  302.6 8.2 fusion.86
  310.8 32.8 %all-gather.15.cloned.1.call-done = bf16[768,3072]{1,0:T(8,128)(2,1)} async-done(((bf16[768,384]{1,0:T(8,128)(2,1)}), bf16[768,3072]{1,0:T(8,128)(2,1)}) %all-gather.15.cloned.1.call-update) | async-done | bytes 4718608 | tf_op jit(solution)/shard_map/all_gather | solution.py:312
  343.7 5.3 fusion.30
  349.7 6.4 multiply_reduce_fusion.5
  367.0 5.2 fusion.21
  372.2 5.9 fusion.82
  381.0 4.1 fusion.43
  386.8 5.1 fusion.39
  393.9 6.3 fusion.54
  401.7 3.5 fusion.32
  406.8 6.0 broadcast_multiply_fusion
  413.0 60.3 %reduce-scatter.8.cloned.1.call-done = f32[768,288]{0,1:T(8,128)} async-done(((f32[768,2304]{0,1:T(8,128)}), f32[768,288]{0,1:T(8,128)}) %reduce-scatter.8.cloned.1.call-update) | async-done | bytes 884752 | tf_op jit(solution)/shard_map/reduce_scatter | solution.py:321
  473.3 100.2 %reduce-scatter.12.cloned.1.call-done = f32[768,384]{1,0:T(8,128)} async-done(((f32[768,3072]{1,0:T(8,128)}), f32[768,384]{1,0:T(8,128)}) %reduce-scatter.12.cloned.1.call-update) | async-done | bytes 1179664 | tf_op jit(solution)/shard_map/reduce_scatter | solution.py:326
  573.5 100.2 %reduce-scatter.14.cloned.1.call-done = f32[3072,96]{0,1:T(8,128)} async-done(((f32[3072,768]{0,1:T(8,128)}), f32[3072,96]{0,1:T(8,128)}) %reduce-scatter.14.cloned.1.call-update) | async-done | bytes 1179664 | tf_op jit(solution)/shard_map/reduce_scatter | solution.py:328
  673.7 144.7 %reduce-scatter.6.cloned.1.call-done = f32[768,576]{0,1:T(8,128)} async-done(((f32[768,4608]{0,1:T(8,128)}), f32[768,576]{0,1:T(8,128)}) %reduce-scatter.6.cloned.1.call-update) | async-done | bytes 1769488 | tf_op jit(solution)/shard_map/reduce_scatter | solution.py:319
  820.7 26.4 %all-reduce.11 = (f32[4608]{0:T(1024)S(1)}, f32[768]{0:T(1024)S(1)}, f32[768]{0:T(1024)S(1)}, f32[768]{0:T(1024)S(1)}, f32[3072]{0:T(1024)S(1)}, /*index=5*/f32[768]{0:T(1024)S(1)}) all-reduce(f32[4608]{0:T(1024)S(1)} %reduce.38, f32[768]{0:T(1024)S(1)} %reduce_sum.235, ...), channel_id=3, replica_groups=mesh['rep'=4,'shard'=8] {'shard'}, use_global_device_ids=true, to_apply=%region_19.20.clone | all-reduce | flops 10752 | bytes 86016
  847.5 11.3 %all-reduce.12 = (f32[576]{0:T(1024)}, f32[96]{0:T(128)}, f32[96]{0:T(128)}, f32[96]{0:T(128)}, f32[384]{0:T(512)}, /*index=5*/f32[96]{0:T(128)}) all-reduce(f32[576]{0:T(1024)S(1)} %dynamic-slice.6, f32[96]{0:T(128)S(1)} %dynamic-slice.8, f32[96]{0:T(128)S(1)} %dynamic-slice.10, ...), channel_id=1, replica_groups=mesh['rep'=4,'shard'=8] {'rep'}, use_global_device_ids=true, to_apply=%region_20.21 | all-reduce | flops 1344 | bytes 10752 | tf_op jit(solution)/shard_map/psum | solution.py:331
  860.0 4.6 fusion.24
  864.6 79.2 %all-reduce.17.cloned.1.call-done = (f32[768,576]{0,1:T(8,128)}, f32[768,288]{0,1:T(8,128)}, f32[768,96]{0,1:T(8,128)}, f32[768,384]{1,0:T(8,128)}, f32[3072,96]{0,1:T(8,128)}) async-done(((f32[768,576]{0,1:T(8,128)}, f32[768,288]{0,1:T(8,128)}, f32[768,96]{0,1:T(8,128)}, f32[768,384]{1,0:T(8,128)}, f32[3072,96]{0,1:T(8,128)}), (f32[768,576]{0,1:T(8,128)}, f32[768,288]{0,1:T(8,128)}, f32[768,96]{0,1:T(8,128)}, ...) | async-done | bytes 5308432 | tf_op jit(solution)/shard_map/psum | solution.py:331
  (252 shorter events, 72.3 us)
Async XLA Ops:
  7.2 271.1 %all-gather.7.cloned.1.call-start = ((), (), s32[]{:S(2)}) async-start(), calls=%async_computation.5 | async-start | bytes 7962624 | tf_op jit(solution)/shard_map/all_gather | solution.py:291
  7.9 276.1 %all-gather.9.cloned.1.call-start = ((), (), s32[]{:S(2)}) async-start(), calls=%async_computation.6 | async-start | bytes 3981312 | tf_op jit(solution)/shard_map/all_gather | solution.py:293
  8.7 284.4 %all-gather.11.cloned.1.call-start = ((), (), s32[]{:S(2)}) async-start(), calls=%async_computation.7 | async-start | bytes 1327104 | tf_op jit(solution)/shard_map/all_gather | solution.py:296
  9.4 293.2 %all-gather.13.cloned.1.call-start = ((), (), s32[]{:S(2)}) async-start(), calls=%async_computation.8 | async-start | bytes 5308416 | tf_op jit(solution)/shard_map/all_gather | solution.py:300
  10.0 333.6 %all-gather.15.cloned.1.call-start = ((), (), s32[]{:S(2)}) async-start(), calls=%async_computation.9 | async-start | bytes 5308416 | tf_op jit(solution)/shard_map/all_gather | solution.py:312
  10.0 2.4 collective-permute-start
  13.9 78.2 %collective-permute-start.1 = (bf16[2,768,384]{2,1,0:T(8,128)(2,1)S(1)}, bf16[2,768,384]{2,1,0:T(8,128)(2,1)S(1)}, u32[]{:S(2)}, u32[]{:S(2)}) collective-permute-start(bf16[2,768,384]{2,1,0:T(8,128)(2,1)S(1)} %get-tuple-element.60), channel_id=1, source_target_pairs={{0,2},{1,3},{2,0},{3,1},{4,6},{5,7},{6,4},{7,5},{8,10},{9,11},{10,... | collective-permute-start | bytes 3538952 | tf_op jit(solution)/shard_map/ppermute | solution.py:29
  16.9 396.0 %reduce-scatter.10.cloned.1.call-start = ((), (), s32[]{:S(2)}) async-start(), calls=%async_computation.12 | async-start | bytes 2654208 | tf_op jit(solution)/shard_map/reduce_scatter | solution.py:324
  93.0 161.6 %copy-start.58 = (bf16[384]{0:T(512)(128)(2,1)S(1)}, bf16[384]{0:T(512)(128)(2,1)}, u32[]{:S(2)}) copy-start(bf16[384]{0:T(512)(128)(2,1)} %param.25) | copy-start | bytes 2308
  93.0 176.2 %copy-start = (f32[1,256,768]{2,1,0:T(8,128)S(1)}, f32[1,256,768]{2,1,0:T(8,128)}, u32[]{:S(2)}) copy-start(f32[1,256,768]{2,1,0:T(8,128)} %param.14) | copy-start | bytes 2359300
  95.6 176.6 %collective-permute-start.2 = (bf16[4,768,384]{1,2,0:T(8,128)(2,1)}, bf16[4,768,384]{1,2,0:T(8,128)(2,1)}, u32[]{:S(2)}, u32[]{:S(2)}) collective-permute-start(bf16[4,768,384]{1,2,0:T(8,128)(2,1)} %copy.54), channel_id=1, source_target_pairs={{0,4},{1,5},{2,6},{3,7},{4,0},{5,1},{6,2},{7,3},{8,12},{9,13},{10,... | collective-permute-start | bytes 7077896 | tf_op jit(solution)/shard_map/ppermute | solution.py:29
  269.3 14.7 %copy-start.28 = (f32[256]{0:T(256)}, f32[256]{0:T(256)S(1)}, u32[]{:S(2)}) copy-start(f32[256]{0:T(256)S(1)} %broadcast_multiply_fusion.6) | copy-start | bytes 3076
  269.6 14.4 %copy-start.32 = (f32[256]{0:T(256)}, f32[256]{0:T(256)S(1)}, u32[]{:S(2)}) copy-start(f32[256]{0:T(256)S(1)} %add_rsqrt_fusion.1) | copy-start | bytes 3076
  358.9 114.3 %reduce-scatter.8.cloned.1.call-start = ((), (), s32[]{:S(2)}) async-start(), calls=%async_computation.11 | async-start | bytes 7962624 | tf_op jit(solution)/shard_map/reduce_scatter | solution.py:321
  385.2 188.3 %reduce-scatter.12.cloned.1.call-start = ((), (), s32[]{:S(2)}) async-start(), calls=%async_computation.13 | async-start | bytes 10616832 | tf_op jit(solution)/shard_map/reduce_scatter | solution.py:326
  392.0 281.7 %reduce-scatter.14.cloned.1.call-start = ((), (), s32[]{:S(2)}) async-start(), calls=%async_computation.14 | async-start | bytes 10616832 | tf_op jit(solution)/shard_map/reduce_scatter | solution.py:328
  400.3 418.1 %reduce-scatter.6.cloned.1.call-start = ((), (), s32[]{:S(2)}) async-start(), calls=%async_computation.10 | async-start | bytes 15925248 | tf_op jit(solution)/shard_map/reduce_scatter | solution.py:319
  412.8 407.5 %copy-start.52 = (f32[12,64]{1,0:T(8,128)S(1)}, f32[12,64]{1,0:T(8,128)}, u32[]{:S(2)}) copy-start(f32[12,64]{1,0:T(8,128)} %get-tuple-element.67) | copy-start | bytes 9220
  412.8 407.6 %copy-start.36 = (f32[12,64]{1,0:T(8,128)S(1)}, f32[12,64]{1,0:T(8,128)}, u32[]{:S(2)}) copy-start(f32[12,64]{1,0:T(8,128)} %get-tuple-element.65) | copy-start | bytes 9220
  412.9 407.8 %copy-start.48 = (f32[3072]{0:T(1024)S(1)}, f32[3072]{0:T(1024)}, u32[]{:S(2)}) copy-start(f32[3072]{0:T(1024)} %get-tuple-element.78) | copy-start | bytes 36868
  412.9 407.8 %copy-start.53 = (f32[768]{0:T(1024)S(1)}, f32[768]{0:T(1024)}, u32[]{:S(2)}) copy-start(f32[768]{0:T(1024)} %get-tuple-element.18) | copy-start | bytes 9220
  412.9 407.8 %copy-start.54 = (f32[768]{0:T(1024)S(1)}, f32[768]{0:T(1024)}, u32[]{:S(2)}) copy-start(f32[768]{0:T(1024)} %get-tuple-element.63) | copy-start | bytes 9220
  412.9 446.0 %copy-start.4 = (f32[1,256,768]{2,1,0:T(8,128)S(1)}, f32[1,256,768]{2,1,0:T(8,128)}, u32[]{:S(2)}) copy-start(f32[1,256,768]{2,1,0:T(8,128)} %copy-done.3) | copy-start | bytes 2359300
  412.9 530.9 %all-reduce.17.cloned.1.call-start = ((), (), s32[]{:S(2)}) async-start(), calls=%async_computation.15 | async-start | bytes 10616832 | tf_op jit(solution)/shard_map/psum | solution.py:331
  (53 other events, 194.0 us)
Sparse Core Ops, SparseCore 0:
  9.6 92.2 all-gather.6
  103.6 93.7 all-gather.8
  199.0 25.9 all-gather.10
  226.5 65.3 all-gather.12
  293.4 50.2 all-gather.14
  359.1 35.6 reduce-scatter.9
  397.1 76.1 reduce-scatter.7
  475.6 97.8 reduce-scatter.11
  575.8 97.8 reduce-scatter.13
  675.9 142.4 reduce-scatter.5
  822.6 121.1 all-reduce.16
